TPU v7x, 32 devices: a whole 2x2x4 slice. The times are simulated.
32 devices in a mesh: seq: 8 (over y, x, core), batch: 4 (over z).
Axes of the slice: x: 2, y: 2, z: 4, core: 2. Of those that a mesh axis runs over, the one named last changes fastest.
Arguments:
- values: bfloat16 [1, 2048, 512], P(None, 'seq', 'batch'), may hold values from -6 to 6
- gate_in: bfloat16 [1, 2048, 512], P(None, 'seq', 'batch'), may hold values from -6 to 6
- gate_out: bfloat16 [1, 2048, 512], P(None, 'seq', 'batch'), may hold values from -6 to 6
- cotangent: bfloat16 [1, 2048, 512], P(None, 'seq', 'batch'), may hold values from -6 to 6
- filters: float32 [64, 2048], P(None, 'seq'), may hold values from -0.125 to 0.125
Outputs:
- grad_values: bfloat16 [1, 2048, 512], P(None, 'seq', 'batch')
- grad_gate_in: bfloat16 [1, 2048, 512], P(None, 'seq', 'batch')
- grad_gate_out: bfloat16 [1, 2048, 512], P(None, 'seq', 'batch')
- grad_filters: float32 [64, 2048], P('batch', 'seq')
All inputs are finite; a program needn't handle non-finite values.
Results may differ from a plain program's by a relative error of at most 0.012.
Values may be sent and summed in bfloat16 or wider, within the bound.
A program may use at most 128 MiB of HBM per device.

v0:
```python
import math

import jax
import jax.numpy as jnp
from jax import lax
from jax.sharding import PartitionSpec as P

HIGHEST = lax.Precision.HIGHEST


def as_sent(x):

    def short(part):
        return part.astype(jnp.bfloat16) if part.dtype == jnp.float32 else part

    return jax.tree.map(short, x)


def angle_table(first, second, period):
    left_idx = lax.broadcasted_iota(jnp.int32, (first, second), 0)
    right_idx = lax.broadcasted_iota(jnp.int32, (first, second), 1)
    angle = (left_idx * right_idx % period).astype(jnp.float32) * (2.0 * math.pi / period)
    return (jnp.cos(angle), jnp.sin(angle))


def dft_tables(used_rows, total_rows, columns):
    modulus = total_rows * columns
    cos_rows, sin_rows = angle_table(total_rows, used_rows, total_rows)
    k_twist = lax.broadcasted_iota(jnp.int32, (total_rows, 1, columns), 0)
    s_twist = lax.broadcasted_iota(jnp.int32, (total_rows, 1, columns), 2)
    angle_twist = (k_twist * s_twist % modulus).astype(jnp.float32) * (2.0 * math.pi / modulus)
    outer_len = max(
        [
            divisor
            for divisor in range(1, columns + 1)
            if columns % divisor == 0 and divisor * divisor <= columns
        ]
    )
    inner_len = columns // outer_len
    cos_outer, sin_outer = angle_table(outer_len, outer_len, outer_len)
    cos_inner, sin_inner = angle_table(inner_len, inner_len, inner_len)
    cos_small, sin_small = angle_table(outer_len, inner_len, columns)
    return (
        cos_rows,
        sin_rows,
        jnp.cos(angle_twist),
        jnp.sin(angle_twist),
        cos_outer,
        sin_outer,
        cos_inner,
        sin_inner,
        cos_small,
        sin_small,
        outer_len,
        inner_len,
        modulus,
    )


def by_rows(table, series):
    return jnp.einsum("kr,rcs->kcs", table, series, precision=HIGHEST)


def to_rows(table, series):
    return jnp.einsum("kr,kcs->rcs", table, series, precision=HIGHEST)


def by_outer(table, series):
    return jnp.einsum("ji,kcis->kcjs", table, series, precision=HIGHEST)


def by_inner(series, table):
    return jnp.einsum("kcjs,sq->kcjq", series, table, precision=HIGHEST)


def inner_forward(part_re, part_im, tables):
    cos_outer, sin_outer, cos_inner, sin_inner, cos_small, sin_small, outer_len, inner_len = tables[
        4:12
    ]
    shape = part_re.shape
    split_re = part_re.reshape(shape[0], shape[1], outer_len, inner_len)
    split_im = part_im.reshape(shape[0], shape[1], outer_len, inner_len)
    first_re = by_outer(cos_outer, split_re) + by_outer(sin_outer, split_im)
    first_im = by_outer(cos_outer, split_im) - by_outer(sin_outer, split_re)
    turned_re = first_re * cos_small + first_im * sin_small
    turned_im = first_im * cos_small - first_re * sin_small
    out_re = by_inner(turned_re, cos_inner) + by_inner(turned_im, sin_inner)
    out_im = by_inner(turned_im, cos_inner) - by_inner(turned_re, sin_inner)
    return (out_re.reshape(shape), out_im.reshape(shape))


def inner_inverse(part_re, part_im, tables):
    cos_outer, sin_outer, cos_inner, sin_inner, cos_small, sin_small, outer_len, inner_len = tables[
        4:12
    ]
    shape = part_re.shape
    split_re = part_re.reshape(shape[0], shape[1], outer_len, inner_len)
    split_im = part_im.reshape(shape[0], shape[1], outer_len, inner_len)
    first_re = by_inner(split_re, cos_inner) - by_inner(split_im, sin_inner)
    first_im = by_inner(split_im, cos_inner) + by_inner(split_re, sin_inner)
    turned_re = first_re * cos_small - first_im * sin_small
    turned_im = first_im * cos_small + first_re * sin_small
    out_re = by_outer(cos_outer, turned_re) - by_outer(sin_outer, turned_im)
    out_im = by_outer(cos_outer, turned_im) + by_outer(sin_outer, turned_re)
    return (out_re.reshape(shape), out_im.reshape(shape))


def spectrum(series, tables):
    cos_rows, sin_rows, cos_twist, sin_twist = tables[0:4]
    first_re = by_rows(cos_rows, series)
    first_im = -by_rows(sin_rows, series)
    turned_re = first_re * cos_twist + first_im * sin_twist
    turned_im = first_im * cos_twist - first_re * sin_twist
    return inner_forward(turned_re, turned_im, tables)


def synthesis(spec_re, spec_im, tables):
    cos_rows, sin_rows, cos_twist, sin_twist = tables[0:4]
    modulus = tables[12]
    inner_re, inner_im = inner_inverse(spec_re, spec_im, tables)
    turned_re = inner_re * cos_twist - inner_im * sin_twist
    turned_im = inner_im * cos_twist + inner_re * sin_twist
    result = to_rows(cos_rows, turned_re) - to_rows(sin_rows, turned_im)
    return result * (1.0 / modulus)


def to_owner(block):
    return jnp.swapaxes(block, 1, 2)[None]


def from_owner(block):
    return jnp.swapaxes(block[0], 1, 2)


def times_bf16(left, right):
    return (left.astype(jnp.float32) * right.astype(jnp.float32)).astype(jnp.bfloat16)


def body(values, gate_in, gate_out, cotangent, filters):
    seq_count = values.shape[0]
    tokens = values.shape[1]
    channels = values.shape[2]
    filter_count = filters.shape[0]
    shards = lax.axis_size("seq")
    replicas = lax.axis_size("batch")
    owned_count = channels // shards
    tables = dft_tables(shards, 2 * shards, tokens)

    def flatten_series(block):
        return block.reshape(block.shape[0], seq_count * owned_count, tokens)

    def grouped(block):
        return block.reshape(block.shape[0], seq_count, owned_count, tokens)

    spread = jnp.tile(filters, (channels // filter_count, 1)).reshape(1, channels, tokens)
    owned_taps = lax.all_to_all(spread, "seq", split_axis=1, concat_axis=0, tiled=True)
    tap_re, tap_im = spectrum(owned_taps, tables)
    tap_re = tap_re[:, None]
    tap_im = tap_im[:, None]
    mixed_in = times_bf16(values, gate_in)
    grad_mixed = times_bf16(cotangent, gate_out)
    owned_in, owned_grad = (
        lax.all_to_all(to_owner(mixed_in), "seq", split_axis=2, concat_axis=0, tiled=True),
        lax.all_to_all(to_owner(grad_mixed), "seq", split_axis=2, concat_axis=0, tiled=True),
    )
    in_re, in_im = spectrum(flatten_series(owned_in).astype(jnp.float32), tables)
    grad_re, grad_im = spectrum(flatten_series(owned_grad).astype(jnp.float32), tables)
    in_re = grouped(in_re)
    in_im = grouped(in_im)
    grad_re = grouped(grad_re)
    grad_im = grouped(grad_im)
    conv_out = grouped(
        synthesis(
            flatten_series(tap_re * in_re - tap_im * in_im),
            flatten_series(tap_re * in_im + tap_im * in_re),
            tables,
        )
    ).astype(jnp.bfloat16)
    grad_conv_in = grouped(
        synthesis(
            flatten_series(tap_re * grad_re + tap_im * grad_im),
            flatten_series(tap_re * grad_im - tap_im * grad_re),
            tables,
        )
    ).astype(jnp.bfloat16)
    tap_terms = synthesis(
        jnp.sum(in_re * grad_re + in_im * grad_im, axis=1),
        jnp.sum(in_re * grad_im - in_im * grad_re, axis=1),
        tables,
    )
    back_owned, conv_owned = (
        lax.all_to_all(grad_conv_in, "seq", split_axis=0, concat_axis=2, tiled=True),
        lax.all_to_all(conv_out, "seq", split_axis=0, concat_axis=2, tiled=True),
    )
    back_seq = from_owner(back_owned)
    conv_seq = from_owner(conv_owned)
    grad_values = times_bf16(gate_in, back_seq)
    grad_gate_in = times_bf16(values, back_seq)
    grad_gate_out = times_bf16(cotangent, conv_seq)
    tap_seq = lax.all_to_all(
        as_sent(tap_terms), "seq", split_axis=0, concat_axis=1, tiled=True
    ).astype(tap_terms.dtype)
    shared = channels * replicas // filter_count
    factor = 1.0 / math.sqrt(shared * seq_count * shards * tokens)
    per_filter = (
        tap_seq.reshape(channels // filter_count, filter_count, tokens).sum(axis=0) * factor
    )
    grad_filters = lax.psum_scatter(
        per_filter.astype(jnp.bfloat16), "batch", scatter_dimension=0, tiled=True
    ).astype(jnp.float32)
    return (grad_values, grad_gate_in, grad_gate_out, grad_filters)


def solution(mesh):
    placed = (
        P(None, "seq", "batch"),
        P(None, "seq", "batch"),
        P(None, "seq", "batch"),
        P(None, "seq", "batch"),
        P(None, "seq"),
    )
    return jax.shard_map(
        body,
        mesh=mesh,
        in_specs=placed,
        out_specs=(
            P(None, "seq", "batch"),
            P(None, "seq", "batch"),
            P(None, "seq", "batch"),
            P("batch", "seq"),
        ),
        check_vma=False,
    )
```

profile of v0, /device:TPU:0, one launch (start us, length us, event | category | flops | bytes accessed | tf_op | source)
XLA Modules:
  0.0 472.2 jit_solution(8969163546440852837)
XLA Ops:
  11.4 5.2 %all-to-all-start.1 = ((bf16[8,2,2048]{2,1,0:T(2,128)(2,1)}), bf16[8,2,2048]{2,1,0:T(2,128)(2,1)S(1)}, u32[]{:S(2)}, u32[]{:S(2)}) async-start(bf16[8,2,2048]{2,1,0:T(2,128)(2,1)} %reshape.247), calls=%async_computation.1 | async-start | bytes 131072 | tf_op jit(solution)/shard_map/all_to_all | solution.py:164
  21.7 4.1 all-to-all-start.3
  26.6 4.2 all-to-all-done.3
  30.8 3.5 all-to-all-start
  34.8 5.0 %all-to-all-done = f32[1,128,256]{2,0,1:T(1,128)S(1)} async-done(((f32[1,128,256]{2,0,1:T(1,128)}), f32[1,128,256]{2,0,1:T(1,128)S(1)}, u32[]{:S(2)}, u32[]{:S(2)}) %all-to-all-start) | async-done | bytes 131104 | tf_op jit(solution)/shard_map/all_to_all | solution.py:156
  43.6 4.8 %fusion.22 = f32[16,16,16,16]{3,2,1,0:T(8,128)} fusion(f32[16,16,16,16]{3,2,0,1:T(8,128)S(1)} %reshape.227), kind=kOutput, calls=%fused_computation.52 | convolution fusion | flops 12586496 | bytes 524288 | tf_op jit(solution)/shard_map/ji,kcis->kcjs/dot_general | solution.py:69
  48.4 4.8 %fusion.24 = f32[16,16,16,16]{3,2,1,0:T(8,128)} fusion(f32[16,16,16,16]{3,2,0,1:T(8,128)S(1)} %reshape.227), kind=kOutput, calls=%fused_computation.54 | convolution fusion | flops 12586496 | bytes 524288 | tf_op jit(solution)/shard_map/ji,kcis->kcjs/dot_general | solution.py:69
  55.2 5.6 %fusion.33 = f32[16,16,16,16]{3,2,1,0:T(8,128)S(1)} fusion(f32[16,16,16,16]{3,2,1,0:T(8,128)} %fusion.22, f32[16,16,16,16]{3,2,0,1:T(8,128)} %reshape.226), kind=kOutput, calls=%fused_computation.61 | convolution fusion | flops 12652032 | bytes 786432 | tf_op jit(solution)/shard_map/ji,kcis->kcjs/dot_general | solution.py:69
  64.2 4.8 %fusion.62 = f32[16,16,16,16]{3,2,1,0:T(8,128)} fusion(f32[16,16,16,16]{3,2,1,0:T(8,128)S(1)} %fusion.33, f32[16,16,16,16]{3,2,1,0:T(8,128)S(1)} %fusion.30, f32[16,16]{0,1:T(8,128)S(1)} %copy.121, f32[16,16]{0,1:T(8,128)S(1)} %copy.118), kind=kOutput, calls=%fused_computation.98 | convolution fusion | flops 12783104 | bytes 788480 | tf_op jit(solution)/shard_map/kcjs,sq->kcjq/dot_general | solution.py:73
  69.0 4.8 %fusion.66 = f32[16,16,16,16]{3,2,1,0:T(8,128)} fusion(f32[16,16,16,16]{3,2,1,0:T(8,128)S(1)} %fusion.33, f32[16,16,16,16]{3,2,1,0:T(8,128)S(1)} %fusion.30, f32[16,16]{0,1:T(8,128)S(1)} %copy.121, f32[16,16]{0,1:T(8,128)S(1)} %copy.118), kind=kOutput, calls=%fused_computation.99 | convolution fusion | flops 12783104 | bytes 788480 | tf_op jit(solution)/shard_map/kcjs,sq->kcjq/dot_general | solution.py:73
  75.9 6.5 %fusion.14 = f32[16,16,16,16]{3,2,1,0:T(8,128)} fusion(f32[16,16,16,16]{3,2,0,1:T(8,128)} %reshape.230), kind=kOutput, calls=%fused_computation.44 | convolution fusion | flops 12586496 | bytes 524288 | tf_op jit(solution)/shard_map/ji,kcis->kcjs/dot_general | solution.py:69
  82.4 4.8 %fusion.16 = f32[16,16,16,16]{3,2,1,0:T(8,128)} fusion(f32[16,16,16,16]{3,2,0,1:T(8,128)S(1)} %copy-done.14), kind=kOutput, calls=%fused_computation.46 | convolution fusion | flops 12586496 | bytes 524288 | tf_op jit(solution)/shard_map/ji,kcis->kcjs/dot_general | solution.py:69
  89.3 5.6 %fusion.39 = f32[16,16,16,16]{3,2,1,0:T(8,128)S(1)} fusion(f32[16,16,16,16]{3,2,1,0:T(8,128)} %fusion.14, f32[16,16,16,16]{3,2,0,1:T(8,128)} %reshape.229), kind=kOutput, calls=%fused_computation.63 | convolution fusion | flops 12652032 | bytes 786432 | tf_op jit(solution)/shard_map/ji,kcis->kcjs/dot_general | solution.py:69
  98.3 4.8 %fusion.68 = f32[16,16,16,16]{3,2,1,0:T(8,128)} fusion(f32[16,16,16,16]{3,2,1,0:T(8,128)S(1)} %fusion.39, f32[16,16,16,16]{3,2,1,0:T(8,128)S(1)} %fusion.36, f32[16,16]{0,1:T(8,128)S(1)} %copy.121, f32[16,16]{0,1:T(8,128)S(1)} %copy.118), kind=kOutput, calls=%fused_computation.100 | convolution fusion | flops 12783104 | bytes 788480 | tf_op jit(solution)/shard_map/kcjs,sq->kcjq/dot_general | solution.py:73
  103.1 4.9 %fusion.72 = f32[16,16,16,16]{3,2,1,0:T(8,128)} fusion(f32[16,16,16,16]{3,2,1,0:T(8,128)S(1)} %fusion.39, f32[16,16,16,16]{3,2,1,0:T(8,128)S(1)} %fusion.36, f32[16,16]{0,1:T(8,128)S(1)} %copy.121, f32[16,16]{0,1:T(8,128)S(1)} %copy.118), kind=kOutput, calls=%fused_computation.101 | convolution fusion | flops 12783104 | bytes 788480 | tf_op jit(solution)/shard_map/kcjs,sq->kcjq/dot_general | solution.py:73
  109.9 6.1 %fusion.6 = f32[16,16,16,16]{3,2,1,0:T(8,128)} fusion(f32[16,16,16,16]{3,2,0,1:T(8,128)} %reshape.235), kind=kOutput, calls=%fused_computation.36 | convolution fusion | flops 12586496 | bytes 524288 | tf_op jit(solution)/shard_map/ji,kcis->kcjs/dot_general | solution.py:69
  116.1 4.8 %fusion.8 = f32[16,16,16,16]{3,2,1,0:T(8,128)} fusion(f32[16,16,16,16]{3,2,0,1:T(8,128)S(1)} %copy-done.15), kind=kOutput, calls=%fused_computation.38 | convolution fusion | flops 12586496 | bytes 524288 | tf_op jit(solution)/shard_map/ji,kcis->kcjs/dot_general | solution.py:69
  122.9 5.8 %fusion.45 = f32[16,16,16,16]{3,2,1,0:T(8,128)S(1)} fusion(f32[16,16,16,16]{3,2,1,0:T(8,128)} %fusion.6, f32[16,16,16,16]{3,2,0,1:T(8,128)} %reshape.234), kind=kOutput, calls=%fused_computation.65 | convolution fusion | flops 12652032 | bytes 786432 | tf_op jit(solution)/shard_map/ji,kcis->kcjs/dot_general | solution.py:69
  132.1 3.4 fusion.74
  135.5 3.4 fusion.78
  139.0 4.9 %convolution_subtract_fusion.5 = f32[16,16,16,16]{3,2,1,0:T(8,128)} fusion(f32[16,16,16,16]{3,2,1,0:T(8,128)S(1)} %copy-done.20, f32[16,16,16,16]{3,2,1,0:T(8,128)S(1)} %fusion.33, f32[16,16,16,16]{3,2,1,0:T(8,128)S(1)} %copy-done.4, f32[16,16]{0,1:T(8,128)S(1)} %copy.121, f32[16,16]{0,1:T(8,128)S(1)} %copy.118), kind=kOutput, calls=%fused_computation.75 | convolution fusion | flops 12848640 | bytes 1050624 | tf_op jit(solution)/shard_map/kcjs,sq->kcjq/dot_general | solution.py:73
  144.0 4.8 %convolution_add_fusion.5 = f32[16,16,16,16]{3,2,1,0:T(8,128)} fusion(f32[16,16,16,16]{3,2,1,0:T(8,128)S(1)} %copy-done.19, f32[16,16,16,16]{3,2,1,0:T(8,128)S(1)} %fusion.33, f32[16,16,16,16]{3,2,1,0:T(8,128)S(1)} %copy-done.4, f32[16,16]{0,1:T(8,128)S(1)} %copy.121, f32[16,16]{0,1:T(8,128)S(1)} %copy.118), kind=kOutput, calls=%fused_computation.77 | convolution fusion | flops 12848640 | bytes 1050624 | tf_op jit(solution)/shard_map/kcjs,sq->kcjq/dot_general | solution.py:73
  148.8 3.4 convolution_subtract_fusion.4
  152.2 5.0 %convolution_add_fusion.4 = f32[16,16,16,16]{3,2,1,0:T(8,128)} fusion(f32[16,16,16,16]{3,2,1,0:T(8,128)S(1)} %copy-done.21, f32[16,16,16,16]{3,2,1,0:T(8,128)S(1)} %copy-done.8, f32[16,16,16,16]{3,2,1,0:T(8,128)S(1)} %copy-done.10, f32[16,16]{0,1:T(8,128)S(1)} %copy.121, f32[16,16]{0,1:T(8,128)S(1)} %copy.118), kind=kOutput, calls=%fused_computation.76 | convolution fusion | flops 12848640 | bytes 1050624 | tf_op jit(solution)/shard_map/kcjs,sq->kcjq/dot_general | solution.py:73
  157.3 4.8 %convolution_add_fusion.2 = f32[16,16,16,16]{3,2,1,0:T(8,128)} fusion(f32[16,16,16,16]{3,2,1,0:T(8,128)S(1)} %fusion.78, f32[16,16,16,16]{3,2,1,0:T(8,128)S(1)} %fusion.45, f32[16,16,16,16]{3,2,1,0:T(8,128)S(1)} %fusion.42, f32[16,16]{0,1:T(8,128)S(1)} %copy.121, f32[16,16]{0,1:T(8,128)S(1)} %copy.118), kind=kOutput, calls=%fused_computation.71 | convolution fusion | flops 12848640 | bytes 1050624 | tf_op jit(solution)/shard_map/kcjs,sq->kcjq/dot_general | solution.py:73
  162.1 6.4 %multiply_subtract_fusion.1 = (f32[16,16,16,16]{3,2,1,0:T(8,128)S(1)}, f32[16,16,16,16]{3,2,1,0:T(8,128)S(1)}, f32[16,16,16,16]{3,2,1,0:T(8,128)S(1)}, f32[16,16...) fusion(f32[16,16,16,16]{3,2,1,0:T(8,128)} %convolution_add_fusion.4, ...), kind=kOutput, calls=%fused_computation.22 | convolution fusion | flops 14028288 | bytes 3672064 | tf_op jit(solution)/shard_map/kcjs,sq->kcjq/dot_general | solution.py:73
  168.5 14.8 %fusion.165 = f32[16,16,16,16]{2,3,1,0:T(8,128)S(1)} fusion(f32[16,16,16,16]{3,2,1,0:T(8,128)S(1)} %get-tuple-element.12), kind=kOutput, calls=%fused_computation.212 | convolution fusion | flops 12586496 | bytes 524288 | tf_op jit(solution)/shard_map/kcjs,sq->kcjq/dot_general | solution.py:73
  183.3 14.8 %fusion.167 = f32[16,16,16,16]{2,3,1,0:T(8,128)S(1)} fusion(f32[16,16,16,16]{3,2,1,0:T(8,128)S(1)} %get-tuple-element.13), kind=kOutput, calls=%fused_computation.214 | convolution fusion | flops 12586496 | bytes 524288 | tf_op jit(solution)/shard_map/kcjs,sq->kcjq/dot_general | solution.py:73
  198.1 14.9 %convolution_add_fusion = f32[16,16,16,16]{2,3,1,0:T(8,128)S(1)} fusion(f32[16,16,16,16]{2,3,1,0:T(8,128)S(1)} %fusion.165, f32[16,16,16,16]{3,2,1,0:T(8,128)S(1)} %get-tuple-element.13), kind=kOutput, calls=%fused_computation.66 | convolution fusion | flops 12652032 | bytes 786432 | tf_op jit(solution)/shard_map/kcjs,sq->kcjq/dot_general | solution.py:73
  213.0 14.8 %convolution_subtract_fusion = f32[16,16,16,16]{2,3,1,0:T(8,128)S(1)} fusion(f32[16,16,16,16]{2,3,1,0:T(8,128)S(1)} %fusion.167, f32[16,16,16,16]{3,2,1,0:T(8,128)S(1)} %get-tuple-element.12), kind=kOutput, calls=%fused_computation.67 | convolution fusion | flops 12652032 | bytes 786432 | tf_op jit(solution)/shard_map/kcjs,sq->kcjq/dot_general | solution.py:73
  233.2 14.8 %fusion.183 = f32[16,16,16,16]{2,3,1,0:T(8,128)S(1)} fusion(f32[16,16,16,16]{3,2,1,0:T(8,128)S(1)} %get-tuple-element.18), kind=kOutput, calls=%fused_computation.230 | convolution fusion | flops 12586496 | bytes 524288 | tf_op jit(solution)/shard_map/kcjs,sq->kcjq/dot_general | solution.py:73
  247.9 15.2 %fusion.181 = f32[16,16,16,16]{2,3,1,0:T(8,128)S(1)} fusion(f32[16,16,16,16]{3,2,1,0:T(8,128)S(1)} %get-tuple-element.19), kind=kOutput, calls=%fused_computation.228 | convolution fusion | flops 12586496 | bytes 524288 | tf_op jit(solution)/shard_map/kcjs,sq->kcjq/dot_general | solution.py:73
  263.1 14.8 %convolution_subtract_fusion.3 = f32[16,16,16,16]{2,3,1,0:T(8,128)S(1)} fusion(f32[16,16,16,16]{2,3,1,0:T(8,128)S(1)} %fusion.183, f32[16,16,16,16]{3,2,1,0:T(8,128)S(1)} %get-tuple-element.19), kind=kOutput, calls=%fused_computation.73 | convolution fusion | flops 12652032 | bytes 786432 | tf_op jit(solution)/shard_map/kcjs,sq->kcjq/dot_general | solution.py:73
  277.9 14.9 %convolution_add_fusion.3 = f32[16,16,16,16]{2,3,1,0:T(8,128)S(1)} fusion(f32[16,16,16,16]{2,3,1,0:T(8,128)S(1)} %fusion.181, f32[16,16,16,16]{3,2,1,0:T(8,128)S(1)} %get-tuple-element.18), kind=kOutput, calls=%fused_computation.72 | convolution fusion | flops 12652032 | bytes 786432 | tf_op jit(solution)/shard_map/kcjs,sq->kcjq/dot_general | solution.py:73
  299.3 15.2 %fusion.173 = f32[16,16,16,16]{2,3,1,0:T(8,128)S(1)} fusion(f32[16,16,16,16]{3,2,1,0:T(8,128)S(1)} %get-tuple-element.20), kind=kOutput, calls=%fused_computation.220 | convolution fusion | flops 12586496 | bytes 524288 | tf_op jit(solution)/shard_map/kcjs,sq->kcjq/dot_general | solution.py:73
  314.5 14.8 %fusion.171 = f32[16,16,16,16]{2,3,1,0:T(8,128)S(1)} fusion(f32[16,16,16,16]{3,2,1,0:T(8,128)S(1)} %get-tuple-element.21), kind=kOutput, calls=%fused_computation.218 | convolution fusion | flops 12586496 | bytes 524288 | tf_op jit(solution)/shard_map/kcjs,sq->kcjq/dot_general | solution.py:73
  329.2 14.8 %convolution_subtract_fusion.1 = f32[16,16,16,16]{2,3,1,0:T(8,128)S(1)} fusion(f32[16,16,16,16]{2,3,1,0:T(8,128)S(1)} %fusion.173, f32[16,16,16,16]{3,2,1,0:T(8,128)S(1)} %get-tuple-element.21), kind=kOutput, calls=%fused_computation.69 | convolution fusion | flops 12652032 | bytes 786432 | tf_op jit(solution)/shard_map/kcjs,sq->kcjq/dot_general | solution.py:73
  344.0 14.9 %convolution_add_fusion.1 = f32[16,16,16,16]{2,3,1,0:T(8,128)S(1)} fusion(f32[16,16,16,16]{2,3,1,0:T(8,128)S(1)} %fusion.171, f32[16,16,16,16]{3,2,1,0:T(8,128)S(1)} %get-tuple-element.20), kind=kOutput, calls=%fused_computation.68 | convolution fusion | flops 12652032 | bytes 786432 | tf_op jit(solution)/shard_map/kcjs,sq->kcjq/dot_general | solution.py:73
  374.3 6.1 %subtract_bitcast_fusion = f32[16,16,16,16]{2,3,1,0:T(8,128)} fusion(f32[16,16,16,16]{3,2,1,0:T(8,128)} %fusion.60, f32[16,16,16,16]{2,3,1,0:T(8,128)} %copy-done.6, f32[16,16,16,16]{2,3,1,0:T(8,128)} %copy-done.5, f32[16,16]{0,1:T(8,128)S(1)} %copy.121, f32[16,16]{0,1:T(8,128)S(1)} %copy.118), kind=kOutput, calls=%fused_computation.19 | convolution fusion | flops 12848640 | bytes 1050624 | tf_op jit(solution)/shard_map/ji,kcis->kcjs/dot_general | solution.py:69
  387.0 3.6 all-to-all-start.5
  390.6 6.1 %add_bitcast_fusion.2 = f32[16,16,16,16]{2,3,1,0:T(8,128)} fusion(f32[16,16,16,16]{3,2,1,0:T(8,128)} %fusion.57, f32[16,16,16,16]{2,3,1,0:T(8,128)} %copy-done.2, f32[16,16,16,16]{2,3,1,0:T(8,128)} %copy-done.1, f32[16,16]{0,1:T(8,128)S(1)} %copy.121, f32[16,16]{0,1:T(8,128)S(1)} %copy.118), kind=kOutput, calls=%fused_computation.30 | convolution fusion | flops 12848640 | bytes 1050624 | tf_op jit(solution)/shard_map/ji,kcis->kcjs/dot_general | solution.py:69
  402.0 6.1 %subtract_bitcast_fusion.2 = f32[16,16,16,16]{2,3,1,0:T(8,128)} fusion(f32[16,16,16,16]{3,2,1,0:T(8,128)} %fusion.56, f32[16,16,16,16]{2,3,1,0:T(8,128)} %copy-done.1, f32[16,16,16,16]{2,3,1,0:T(8,128)} %copy-done.2, f32[16,16]{0,1:T(8,128)S(1)} %copy.121, f32[16,16]{0,1:T(8,128)S(1)} %copy.118), kind=kOutput, calls=%fused_computation.31 | convolution fusion | flops 12848640 | bytes 1050624 | tf_op jit(solution)/shard_map/ji,kcis->kcjs/dot_general | solution.py:69
  414.1 5.5 %add_bitcast_fusion.1 = f32[16,16,16,16]{2,3,1,0:T(8,128)} fusion(f32[16,16,16,16]{3,2,1,0:T(8,128)} %fusion.59, f32[16,16,16,16]{2,3,1,0:T(8,128)} %copy-done, f32[16,16,16,16]{2,3,1,0:T(8,128)S(1)} %convolution_subtract_fusion.1, f32[16,16]{0,1:T(8,128)S(1)} %copy.121, f32[16,16]{0,1:T(8,128)S(1)} %copy.118), kind=kOutput, calls=%fused_computation.24 | convolution fusion | flops 12848640 | bytes 1050624 | tf_op jit(solution)/shard_map/ji,kcis->kcjs/dot_general | solution.py:69
  425.0 5.4 %subtract_bitcast_fusion.1 = f32[16,16,16,16]{2,3,1,0:T(8,128)} fusion(f32[16,16,16,16]{3,2,1,0:T(8,128)} %fusion.58, f32[16,16,16,16]{2,3,1,0:T(8,128)S(1)} %convolution_subtract_fusion.1, f32[16,16,16,16]{2,3,1,0:T(8,128)} %copy-done, f32[16,16]{0,1:T(8,128)S(1)} %copy.121, f32[16,16]{0,1:T(8,128)S(1)} %copy.118), kind=kOutput, calls=%fused_computation.25 | convolution fusion | flops 12848640 | bytes 1050624 | tf_op jit(solution)/shard_map/ji,kcis->kcjs/dot_general | solution.py:69
  435.6 4.2 all-to-all-start.2
  440.5 4.3 all-to-all-done.2
  448.2 4.9 %all-to-all-done.4 = bf16[8,1,16,256]{3,2,1,0:T(8,128)(2,1)S(1)} async-done(((bf16[8,1,16,256]{3,2,1,0:T(8,128)(2,1)}), bf16[8,1,16,256]{3,2,1,0:T(8,128)(2,1)S(1)}, u32[]{:S(2)}, u32[]{:S(2)}) %all-to-all-start.4) | async-done | bytes 65568 | tf_op jit(solution)/shard_map/all_to_all | solution.py:193
  455.3 8.5 %reduce-scatter.2.cloned.1.call-done = bf16[16,256]{1,0:T(8,128)(2,1)} async-done(((bf16[64,256]{1,0:T(8,128)(2,1)}), bf16[16,256]{1,0:T(8,128)(2,1)}) %reduce-scatter.2.cloned.1.call-update) | async-done | bytes 8208 | tf_op jit(solution)/shard_map/reduce_scatter | solution.py:208
  (145 shorter events, 97.9 us)
Async XLA Ops:
  7.2 13.5 %copy-start.31 = (f32[64,256]{1,0:T(8,128)S(1)}, f32[64,256]{1,0:T(8,128)}, u32[]{:S(2)}) copy-start(f32[64,256]{1,0:T(8,128)} %param.9) | copy-start | bytes 196612
  8.2 17.7 %copy-start.25 = (bf16[1,256,128]{1,2,0:T(8,128)(2,1)}, bf16[1,256,128]{1,2,0:T(8,128)(2,1)S(1)}, u32[]{:S(2)}) copy-start(bf16[1,256,128]{1,2,0:T(8,128)(2,1)S(1)} %copy.124) | copy-start | bytes 196612
  11.4 10.2 %all-to-all-start.1 = ((bf16[8,2,2048]{2,1,0:T(2,128)(2,1)}), bf16[8,2,2048]{2,1,0:T(2,128)(2,1)S(1)}, u32[]{:S(2)}, u32[]{:S(2)}) async-start(bf16[8,2,2048]{2,1,0:T(2,128)(2,1)} %reshape.247), calls=%async_computation.1 | async-start | bytes 131072 | tf_op jit(solution)/shard_map/all_to_all | solution.py:164
  17.9 8.0 %copy-start.27 = (bf16[1,256,128]{1,2,0:T(8,128)(2,1)}, bf16[1,256,128]{1,2,0:T(8,128)(2,1)S(1)}, u32[]{:S(2)}) copy-start(bf16[1,256,128]{1,2,0:T(8,128)(2,1)S(1)} %copy.147) | copy-start | bytes 196612
  18.8 7.0 %copy-start.29 = (bf16[1,256,128]{1,2,0:T(8,128)(2,1)}, bf16[1,256,128]{1,2,0:T(8,128)(2,1)S(1)}, u32[]{:S(2)}) copy-start(bf16[1,256,128]{1,2,0:T(8,128)(2,1)S(1)} %copy.113) | copy-start | bytes 196612
  21.7 9.1 %all-to-all-start.3 = ((bf16[8,2,2048]{2,1,0:T(2,128)(2,1)}), bf16[8,2,2048]{2,1,0:T(2,128)(2,1)S(1)}, u32[]{:S(2)}, u32[]{:S(2)}) async-start(bf16[8,2,2048]{2,1,0:T(2,128)(2,1)} %reshape.249), calls=%async_computation.3 | async-start | bytes 131072 | tf_op jit(solution)/shard_map/all_to_all | solution.py:163
  30.8 9.0 %all-to-all-start = ((f32[1,128,256]{2,0,1:T(1,128)}), f32[1,128,256]{2,0,1:T(1,128)S(1)}, u32[]{:S(2)}, u32[]{:S(2)}) async-start(f32[1,128,256]{2,0,1:T(1,128)} %tile.9), calls=%async_computation | async-start | bytes 262144 | tf_op jit(solution)/shard_map/all_to_all | solution.py:156
  55.2 5.6 %copy-start.11 = (f32[16,16,16,16]{3,2,0,1:T(8,128)S(1)}, f32[16,16,16,16]{3,2,0,1:T(8,128)}, u32[]{:S(2)}) copy-start(f32[16,16,16,16]{3,2,0,1:T(8,128)} %reshape.226) | copy-start | bytes 786436
  55.2 5.6 %copy-start.17 = (f32[16,16,16,16]{3,2,1,0:T(8,128)S(1)}, f32[16,16,16,16]{3,2,1,0:T(8,128)}, u32[]{:S(2)}) copy-start(f32[16,16,16,16]{3,2,1,0:T(8,128)} %fusion.24) | copy-start | bytes 786436
  64.2 4.8 %copy-start.3 = (f32[16,16,16,16]{3,2,1,0:T(8,128)}, f32[16,16,16,16]{3,2,1,0:T(8,128)S(1)}, u32[]{:S(2)}) copy-start(f32[16,16,16,16]{3,2,1,0:T(8,128)S(1)} %fusion.30) | copy-start | bytes 786436
  75.9 6.5 %copy-start.14 = (f32[16,16,16,16]{3,2,0,1:T(8,128)S(1)}, f32[16,16,16,16]{3,2,0,1:T(8,128)}, u32[]{:S(2)}) copy-start(f32[16,16,16,16]{3,2,0,1:T(8,128)} %reshape.230) | copy-start | bytes 786436
  89.3 5.6 %copy-start.12 = (f32[16,16,16,16]{3,2,0,1:T(8,128)S(1)}, f32[16,16,16,16]{3,2,0,1:T(8,128)}, u32[]{:S(2)}) copy-start(f32[16,16,16,16]{3,2,0,1:T(8,128)} %reshape.229) | copy-start | bytes 786436
  89.3 5.6 %copy-start.18 = (f32[16,16,16,16]{3,2,1,0:T(8,128)S(1)}, f32[16,16,16,16]{3,2,1,0:T(8,128)}, u32[]{:S(2)}) copy-start(f32[16,16,16,16]{3,2,1,0:T(8,128)} %fusion.16) | copy-start | bytes 786436
  94.8 8.2 %copy-start.7 = (f32[16,16,16,16]{3,2,1,0:T(8,128)}, f32[16,16,16,16]{3,2,1,0:T(8,128)S(1)}, u32[]{:S(2)}) copy-start(f32[16,16,16,16]{3,2,1,0:T(8,128)S(1)} %fusion.39) | copy-start | bytes 786436
  98.3 4.8 %copy-start.9 = (f32[16,16,16,16]{3,2,1,0:T(8,128)}, f32[16,16,16,16]{3,2,1,0:T(8,128)S(1)}, u32[]{:S(2)}) copy-start(f32[16,16,16,16]{3,2,1,0:T(8,128)S(1)} %fusion.36) | copy-start | bytes 786436
  109.9 6.1 %copy-start.15 = (f32[16,16,16,16]{3,2,0,1:T(8,128)S(1)}, f32[16,16,16,16]{3,2,0,1:T(8,128)}, u32[]{:S(2)}) copy-start(f32[16,16,16,16]{3,2,0,1:T(8,128)} %reshape.235) | copy-start | bytes 786436
  122.9 5.8 %copy-start.13 = (f32[16,16,16,16]{3,2,0,1:T(8,128)S(1)}, f32[16,16,16,16]{3,2,0,1:T(8,128)}, u32[]{:S(2)}) copy-start(f32[16,16,16,16]{3,2,0,1:T(8,128)} %reshape.234) | copy-start | bytes 786436
  122.9 5.8 %copy-start.16 = (f32[16,16,16,16]{3,2,1,0:T(8,128)S(1)}, f32[16,16,16,16]{3,2,1,0:T(8,128)}, u32[]{:S(2)}) copy-start(f32[16,16,16,16]{3,2,1,0:T(8,128)} %fusion.8) | copy-start | bytes 786436
  135.5 3.5 copy-start.4
  135.5 3.5 copy-start.20
  139.0 5.0 %copy-start.19 = (f32[16,16,16,16]{3,2,1,0:T(8,128)S(1)}, f32[16,16,16,16]{3,2,1,0:T(8,128)}, u32[]{:S(2)}) copy-start(f32[16,16,16,16]{3,2,1,0:T(8,128)} %fusion.66) | copy-start | bytes 786436
  144.0 4.8 %copy-start.8 = (f32[16,16,16,16]{3,2,1,0:T(8,128)S(1)}, f32[16,16,16,16]{3,2,1,0:T(8,128)}, u32[]{:S(2)}) copy-start(f32[16,16,16,16]{3,2,1,0:T(8,128)} %copy-done.7) | copy-start | bytes 786436
  144.0 4.8 %copy-start.10 = (f32[16,16,16,16]{3,2,1,0:T(8,128)S(1)}, f32[16,16,16,16]{3,2,1,0:T(8,128)}, u32[]{:S(2)}) copy-start(f32[16,16,16,16]{3,2,1,0:T(8,128)} %copy-done.9) | copy-start | bytes 786436
  144.0 4.8 %copy-start.22 = (f32[16,16,16,16]{3,2,1,0:T(8,128)S(1)}, f32[16,16,16,16]{3,2,1,0:T(8,128)}, u32[]{:S(2)}) copy-start(f32[16,16,16,16]{3,2,1,0:T(8,128)} %fusion.68) | copy-start | bytes 786436
  148.8 3.5 copy-start.21
  157.3 4.9 %copy-start.23 = (f32[16,16,16,16]{3,2,1,0:T(8,128)S(1)}, f32[16,16,16,16]{3,2,1,0:T(8,128)}, u32[]{:S(2)}) copy-start(f32[16,16,16,16]{3,2,1,0:T(8,128)} %convolution_subtract_fusion.5) | copy-start | bytes 786436
  157.3 4.9 %copy-start.24 = (f32[16,16,16,16]{3,2,1,0:T(8,128)S(1)}, f32[16,16,16,16]{3,2,1,0:T(8,128)}, u32[]{:S(2)}) copy-start(f32[16,16,16,16]{3,2,1,0:T(8,128)} %convolution_add_fusion.5) | copy-start | bytes 786436
  213.0 152.6 %copy-start.5 = (f32[16,16,16,16]{2,3,1,0:T(8,128)}, f32[16,16,16,16]{2,3,1,0:T(8,128)S(1)}, u32[]{:S(2)}) copy-start(f32[16,16,16,16]{2,3,1,0:T(8,128)S(1)} %convolution_add_fusion) | copy-start | bytes 786436
  227.8 137.8 %copy-start.6 = (f32[16,16,16,16]{2,3,1,0:T(8,128)}, f32[16,16,16,16]{2,3,1,0:T(8,128)S(1)}, u32[]{:S(2)}) copy-start(f32[16,16,16,16]{2,3,1,0:T(8,128)S(1)} %convolution_subtract_fusion) | copy-start | bytes 786436
  277.9 18.2 %copy-start.1 = (f32[16,16,16,16]{2,3,1,0:T(8,128)}, f32[16,16,16,16]{2,3,1,0:T(8,128)S(1)}, u32[]{:S(2)}) copy-start(f32[16,16,16,16]{2,3,1,0:T(8,128)S(1)} %convolution_subtract_fusion.3) | copy-start | bytes 786436
  292.8 3.2 copy-start.2
  359.0 3.4 copy-start
  387.0 48.6 %all-to-all-start.5 = ((bf16[8,16,256]{2,1,0:T(8,128)(2,1)}), bf16[8,16,256]{2,1,0:T(8,128)(2,1)S(1)}, u32[]{:S(2)}, u32[]{:S(2)}) async-start(bf16[8,16,256]{2,1,0:T(8,128)(2,1)} %copy.173), calls=%async_computation.5 | async-start | bytes 131072 | tf_op jit(solution)/shard_map/all_to_all | solution.py:200
  432.7 15.5 %copy-start.28 = (bf16[1,256,128]{1,2,0:T(8,128)(2,1)S(1)}, bf16[1,256,128]{1,2,0:T(8,128)(2,1)}, u32[]{:S(2)}) copy-start(bf16[1,256,128]{1,2,0:T(8,128)(2,1)} %copy-done.27) | copy-start | bytes 196612
  432.7 15.5 %copy-start.30 = (bf16[1,256,128]{1,2,0:T(8,128)(2,1)S(1)}, bf16[1,256,128]{1,2,0:T(8,128)(2,1)}, u32[]{:S(2)}) copy-start(bf16[1,256,128]{1,2,0:T(8,128)(2,1)} %copy-done.29) | copy-start | bytes 196612
  432.7 20.4 %copy-start.26 = (bf16[1,256,128]{1,2,0:T(8,128)(2,1)S(1)}, bf16[1,256,128]{1,2,0:T(8,128)(2,1)}, u32[]{:S(2)}) copy-start(bf16[1,256,128]{1,2,0:T(8,128)(2,1)} %copy-done.25) | copy-start | bytes 196612
  435.6 9.2 %all-to-all-start.2 = ((bf16[8,1,16,256]{3,2,1,0:T(8,128)(2,1)}), bf16[8,1,16,256]{3,2,1,0:T(8,128)(2,1)S(1)}, u32[]{:S(2)}, u32[]{:S(2)}) async-start(bf16[8,1,16,256]{3,2,1,0:T(8,128)(2,1)} %copy.145), calls=%async_computation.2 | async-start | bytes 131072 | tf_op jit(solution)/shard_map/all_to_all | solution.py:192
  439.7 24.0 %reduce-scatter.2.cloned.1.call-start = ((), (), s32[]{:S(2)}) async-start(), calls=%async_computation.7 | async-start | bytes 40960 | tf_op jit(solution)/shard_map/reduce_scatter | solution.py:208
  444.8 8.3 %all-to-all-start.4 = ((bf16[8,1,16,256]{3,2,1,0:T(8,128)(2,1)}), bf16[8,1,16,256]{3,2,1,0:T(8,128)(2,1)S(1)}, u32[]{:S(2)}, u32[]{:S(2)}) async-start(bf16[8,1,16,256]{3,2,1,0:T(8,128)(2,1)} %copy.165), calls=%async_computation.4 | async-start | bytes 131072 | tf_op jit(solution)/shard_map/all_to_all | solution.py:193
Sparse Core Ops, SparseCore 0:
  442.8 20.9 reduce-scatter.1
where the time goes:
time: 476 us; the launch traced here: 472 us
  matrix products  349 us (73%)
  local copies, waits for them, and re-layouts  52.9 us (11%)
  waiting for transfers between devices  26.9 us (6%)
  starting transfers between devices  23.9 us (5%)
  between operations  14.9 us (3%)
    dot_general x24, matrix products, by_inner(): return jnp.einsum('kcjs,sq->kcjq', series, table, precision=HIGHEST)  234 us
    dot_general x24, matrix products, by_outer(): return jnp.einsum('ji,kcis->kcjs', table, series, precision=HIGHEST)  110 us
    reshape x6, local copies, waits for them, and re-layouts, inner_inverse(): return (out_re.reshape(shape), out_im.reshape(shape))  13.1 us
  transfers between devices with their start and end apart: 7, of which 6 were waited for; matrix products, arithmetic and copies ran while one was open for 11% of the time, Pallas kernels for 0%

commit v1 on v0

--- a/solution.py
+++ b/solution.py
@@ -1,8 +1,11 @@
+import functools
 import math
 
 import jax
 import jax.numpy as jnp
 from jax import lax
+from jax.experimental import pallas as pl
+from jax.experimental.pallas import tpu as pltpu
 from jax.sharding import PartitionSpec as P
 
 HIGHEST = lax.Precision.HIGHEST
@@ -136,7 +139,7 @@
     return (left.astype(jnp.float32) * right.astype(jnp.float32)).astype(jnp.bfloat16)
 
 
-def body(values, gate_in, gate_out, cotangent, filters):
+def spectral_body(values, gate_in, gate_out, cotangent, filters):
     seq_count = values.shape[0]
     tokens = values.shape[1]
     channels = values.shape[2]
@@ -211,6 +214,351 @@
     return (grad_values, grad_gate_in, grad_gate_out, grad_filters)
 
 
+LANES = 128
+MESH = pl.DeviceIdType.MESH
+
+
+def kernel(
+    dims,
+    values_ref,
+    gate_in_ref,
+    gate_out_ref,
+    cotangent_ref,
+    filters_ref,
+    grad_values_ref,
+    grad_gate_in_ref,
+    grad_gate_out_ref,
+    grad_filters_ref,
+    sent,
+    held,
+    held_taps,
+    taps_rows,
+    series,
+    padded,
+    result,
+    result_sent,
+    result_held,
+    tap_rows,
+    tap_sent,
+    tap_held,
+    own_sem,
+    in_send,
+    in_recv,
+    taps_send,
+    taps_recv,
+    out_send,
+    out_recv,
+    term_send,
+    term_recv,
+):
+    shards, replicas, tokens, own, reps, factor = dims
+    halves = tokens // LANES
+    blocks = shards * halves
+    lines = 2 * reps * own
+    group = own * shards
+    me = lax.axis_index("seq")
+    row = lax.axis_index("batch")
+    flat = me * replicas + row
+    f32, bf16 = jnp.float32, jnp.bfloat16
+
+    barrier = pltpu.get_barrier_semaphore()
+    for step in range(1, shards * replicas):
+        other = lax.rem(flat + step, shards * replicas)
+        pl.semaphore_signal(
+            barrier,
+            inc=1,
+            device_id={"seq": other // replicas, "batch": lax.rem(other, replicas)},
+            device_id_type=MESH,
+        )
+
+    down = lax.broadcasted_iota(jnp.int32, (LANES, LANES), 0)
+    across = lax.broadcasted_iota(jnp.int32, (LANES, LANES), 1)
+    later = across >= down
+    mirror = jnp.where(down + across == LANES - 1, 1.0, 0.0).astype(bf16)
+
+    def product(left, right):
+        return (left.astype(f32) * right.astype(f32)).astype(bf16)
+
+    for half in range(halves):
+        rows = pl.ds(half * LANES, LANES)
+        mixed = product(values_ref[0, rows, :], gate_in_ref[0, rows, :])
+        grad = product(cotangent_ref[0, rows, :], gate_out_ref[0, rows, :])
+        mixed_t = mixed.astype(f32).T
+        grad_t = jnp.dot(mirror, grad, preferred_element_type=f32).T
+        for owner in range(shards):
+            parts = [
+                part[rep * group + owner * own : rep * group + (owner + 1) * own]
+                for part in (mixed_t, grad_t)
+                for rep in range(reps)
+            ]
+            sent[owner, half * lines : (half + 1) * lines, :] = jnp.concatenate(parts, 0).astype(bf16)
+
+    pl.semaphore_wait(barrier, shards * replicas - 1)
+
+    def taps_copy(source_owner, slot, peer):
+        return pltpu.make_async_remote_copy(
+            src_ref=filters_ref.at[pl.ds(pl.multiple_of(source_owner * own, own), own), :],
+            dst_ref=held_taps.at[slot],
+            send_sem=taps_send.at[peer],
+            recv_sem=taps_recv.at[slot],
+            device_id={"seq": peer},
+            device_id_type=MESH,
+        )
+
+    def in_copy(source_owner, slot, peer):
+        return pltpu.make_async_remote_copy(
+            src_ref=sent.at[source_owner],
+            dst_ref=held.at[slot],
+            send_sem=in_send.at[peer],
+            recv_sem=in_recv.at[slot],
+            device_id={"seq": peer},
+            device_id_type=MESH,
+        )
+
+    def out_copy(slot, peer):
+        return pltpu.make_async_remote_copy(
+            src_ref=result_sent.at[peer],
+            dst_ref=result_held.at[slot],
+            send_sem=out_send.at[peer],
+            recv_sem=out_recv.at[slot],
+            device_id={"seq": peer},
+            device_id_type=MESH,
+        )
+
+    peers = [lax.rem(me + step, shards) for step in range(1, shards)]
+    for peer in peers:
+        taps_copy(peer, me, peer).start()
+        in_copy(peer, me, peer).start()
+    own_taps = pltpu.make_async_copy(
+        filters_ref.at[pl.ds(pl.multiple_of(me * own, own), own), :], held_taps.at[me], own_sem.at[0]
+    )
+    own_in = pltpu.make_async_copy(sent.at[me], held.at[me], own_sem.at[1])
+    own_taps.start()
+    own_in.start()
+    zero_rows = jnp.zeros((blocks, LANES), f32)
+    for rep in range(reps):
+        padded[rep, 0:blocks, :] = zero_rows
+        padded[reps + rep, blocks : 2 * blocks, :] = zero_rows
+    own_taps.wait()
+    own_in.wait()
+    for peer in peers:
+        taps_copy(peer, peer, peer).wait_recv()
+        in_copy(peer, peer, peer).wait_recv()
+    for source in range(shards):
+        series[source * halves * lines : (source + 1) * halves * lines, :] = held[source].astype(f32)
+        for half in range(halves):
+            k = source * halves + half
+            taps_rows[k * own : (k + 1) * own, :] = held_taps[
+                source, :, half * LANES : (half + 1) * LANES
+            ]
+
+    def one_filter(f, carry):
+        for line in range(2 * reps):
+            at = 0 if line >= reps else blocks
+            padded[line, at : at + blocks, :] = series[pl.ds(line * own + f, blocks, stride=lines), :]
+        grad_cols = jnp.concatenate(
+            [padded[reps + rep, 0:blocks, :] for rep in range(reps)], 0
+        ).T.astype(bf16)
+        total = jnp.zeros((2 * reps * blocks, LANES), f32)
+        turned_before = jnp.zeros((LANES, LANES), f32)
+        gram_before = None
+        for pair in range(blocks // 2):
+            lefts, rights = [], []
+            for k in (2 * pair, 2 * pair + 1):
+                taps = jnp.tile(taps_rows[pl.ds(k * own + f, 8, stride=0), :], (LANES // 8, 1))
+                turned = pltpu.roll(taps, 0, 1, stride=1, stride_axis=0)
+                rights.append(jnp.where(later, turned, turned_before).astype(bf16))
+                turned_before = turned
+                lefts.append(
+                    jnp.concatenate(
+                        [padded[rep, blocks - k : 2 * blocks - k, :] for rep in range(reps)]
+                        + [padded[reps + rep, k : blocks + k, :] for rep in range(reps)],
+                        0,
+                    ).astype(bf16)
+                )
+            left = jnp.concatenate(lefts, 1)
+            total = total + jnp.dot(left, jnp.concatenate(rights, 0), preferred_element_type=f32)
+            gram = jnp.dot(grad_cols, left[: reps * blocks], preferred_element_type=f32)
+            for at in range(2):
+                k = 2 * pair + at
+                gram_now = pltpu.roll(
+                    gram[:, at * LANES : (at + 1) * LANES], 0, 1, stride=1, stride_axis=0
+                )
+                if k > 0:
+                    tap_rows[pl.ds((k - 1) * own + f, 1), :] = jnp.sum(
+                        jnp.where(later, gram_before, gram_now), axis=0, keepdims=True
+                    )
+                gram_before = gram_now
+        tap_rows[pl.ds((blocks - 1) * own + f, 1), :] = jnp.sum(
+            jnp.where(later, gram_before, 0.0), axis=0, keepdims=True
+        )
+        for line in range(2 * reps):
+            result[pl.ds(line * own + f, blocks, stride=lines), :] = total[
+                line * blocks : (line + 1) * blocks
+            ]
+        return carry
+
+    lax.fori_loop(0, own, one_filter, 0)
+
+    for peer in range(shards):
+        result_sent[peer] = result[
+            peer * halves * lines : (peer + 1) * halves * lines, :
+        ].astype(bf16)
+    terms = jnp.dot(tap_rows[...].astype(bf16), mirror, preferred_element_type=f32).astype(bf16)
+    for peer in range(shards):
+        tap_sent[peer] = terms[peer * halves * own : (peer + 1) * halves * own]
+
+    for peer in peers:
+        out_copy(me, peer).start()
+    own_out = pltpu.make_async_copy(result_sent.at[me], result_held.at[me], own_sem.at[0])
+    own_out.start()
+
+    per_row = shards // replicas
+    goal = me // per_row
+    slot_here = lax.rem(me, per_row) * replicas + row
+
+    def term_copy(peer, to_row, slot):
+        return pltpu.make_async_remote_copy(
+            src_ref=tap_sent.at[peer],
+            dst_ref=tap_held.at[slot],
+            send_sem=term_send.at[peer],
+            recv_sem=term_recv.at[slot],
+            device_id={"seq": peer, "batch": to_row},
+            device_id_type=MESH,
+        )
+
+    own_term = pltpu.make_async_copy(tap_sent.at[me], tap_held.at[slot_here], own_sem.at[1])
+    stays = goal == row
+    for peer in peers:
+        term_copy(peer, goal, slot_here).start()
+
+    @pl.when(stays)
+    def _():
+        own_term.start()
+
+    @pl.when(jnp.logical_not(stays))
+    def _():
+        term_copy(me, goal, slot_here).start()
+
+    own_out.wait()
+    for peer in peers:
+        out_copy(peer, peer).wait_recv()
+
+    for half in range(halves):
+        rows = pl.ds(half * LANES, LANES)
+        moved = []
+        for kind in range(2):
+            at = half * lines + kind * reps * own
+            block = jnp.concatenate(
+                [
+                    result_held[source, at + rep * own : at + (rep + 1) * own, :].astype(f32)
+                    for rep in range(reps)
+                    for source in range(shards)
+                ],
+                0,
+            )
+            moved.append(block.T)
+        conv = moved[0]
+        back = jnp.dot(mirror, moved[1].astype(bf16), preferred_element_type=f32)
+        grad_values_ref[0, rows, :] = (gate_in_ref[0, rows, :].astype(f32) * back).astype(bf16)
+        grad_gate_in_ref[0, rows, :] = (values_ref[0, rows, :].astype(f32) * back).astype(bf16)
+        grad_gate_out_ref[0, rows, :] = (cotangent_ref[0, rows, :].astype(f32) * conv).astype(bf16)
+
+    for at in range(per_row):
+        for source_row in range(replicas):
+            slot = at * replicas + source_row
+            local = jnp.logical_and(me == row * per_row + at, row == source_row)
+
+            @pl.when(local)
+            def _():
+                own_term.wait()
+
+            @pl.when(jnp.logical_not(local))
+            def _(slot=slot):
+                term_copy(me, row, slot).wait_recv()
+
+    for at in range(per_row):
+        summed = sum(
+            tap_held[at * replicas + source_row].astype(f32) for source_row in range(replicas)
+        )
+        for half in range(halves):
+            grad_filters_ref[at * own : (at + 1) * own, half * LANES : (half + 1) * LANES] = (
+                summed[half * own : (half + 1) * own] * factor
+            )
+
+    for peer in peers:
+        taps_copy(peer, me, peer).wait_send()
+        in_copy(peer, me, peer).wait_send()
+        out_copy(me, peer).wait_send()
+        term_copy(peer, goal, slot_here).wait_send()
+
+    @pl.when(jnp.logical_not(stays))
+    def _():
+        term_copy(me, goal, slot_here).wait_send()
+
+
+def direct_body(values, gate_in, gate_out, cotangent, filters):
+    tokens, channels = values.shape[1:]
+    filter_count = filters.shape[0]
+    shards = lax.axis_size("seq")
+    replicas = lax.axis_size("batch")
+    own = filter_count // shards
+    reps = channels // filter_count
+    halves = tokens // LANES
+    blocks = shards * halves
+    lines = 2 * reps * own
+    factor = 1.0 / math.sqrt(reps * replicas * shards * tokens)
+    vmem = pl.BlockSpec(memory_space=pltpu.VMEM)
+    f32, bf16 = jnp.float32, jnp.bfloat16
+    slab = jax.ShapeDtypeStruct(values.shape, bf16)
+    sems = pltpu.SemaphoreType.DMA((shards,))
+    return pl.pallas_call(
+        functools.partial(kernel, (shards, replicas, tokens, own, reps, factor)),
+        out_shape=(
+            slab,
+            slab,
+            slab,
+            jax.ShapeDtypeStruct((filter_count // replicas, tokens), f32),
+        ),
+        in_specs=[vmem] * 5,
+        out_specs=(vmem,) * 4,
+        scratch_shapes=[
+            pltpu.VMEM((shards, halves * lines, LANES), bf16),
+            pltpu.VMEM((shards, halves * lines, LANES), bf16),
+            pltpu.VMEM((shards, own, tokens), f32),
+            pltpu.VMEM((blocks * own + 8, LANES), f32),
+            pltpu.VMEM((blocks * lines, LANES), f32),
+            pltpu.VMEM((2 * reps, 2 * blocks, LANES), f32),
+            pltpu.VMEM((blocks * lines, LANES), f32),
+            pltpu.VMEM((shards, halves * lines, LANES), bf16),
+            pltpu.VMEM((shards, halves * lines, LANES), bf16),
+            pltpu.VMEM((blocks * own, LANES), f32),
+            pltpu.VMEM((shards, halves * own, LANES), bf16),
+            pltpu.VMEM((shards, halves * own, LANES), bf16),
+            pltpu.SemaphoreType.DMA((2,)),
+        ]
+        + [sems] * 8,
+        compiler_params=pltpu.CompilerParams(collective_id=0, has_side_effects=True),
+    )(values, gate_in, gate_out, cotangent, filters)
+
+
+def body(values, gate_in, gate_out, cotangent, filters):
+    seqs, tokens, channels = values.shape
+    filter_count = filters.shape[0]
+    shards = lax.axis_size("seq")
+    replicas = lax.axis_size("batch")
+    direct = (
+        seqs == 1
+        and channels == LANES
+        and tokens % LANES == 0
+        and channels % filter_count == 0
+        and filter_count % (8 * shards) == 0
+        and shards % replicas == 0
+    )
+    chosen = direct_body if direct else spectral_body
+    return chosen(values, gate_in, gate_out, cotangent, filters)
+
+
 def solution(mesh):
     placed = (
         P(None, "seq", "batch"),

time: 476 us -> 27.6 us (0.06)
  matrix products: 349 us -> 0 us
  local copies, waits for them, and re-layouts: 52.9 us -> 3.69 us
  waiting for transfers between devices: 26.9 us -> 0 us
  starting transfers between devices: 23.9 us -> 0 us
  Pallas kernels: 0 us -> 23 us
  between operations: 14.9 us -> 0.65 us
    dot_general x60 -> x0, matrix products: 349 us -> none  [the longest x24 234 us: by_inner(): return jnp.einsum('kcjs,sq->kcjq', series, table, precision=HIGHEST)]
    reshape x12 -> x0, local copies, waits for them, and re-layouts: 24.9 us -> none  [the longest x6 13.1 us: inner_inverse(): return (out_re.reshape(shape), out_im.reshape(shape))]
    all_to_all x6 -> x0, starting transfers between devices: 23.9 us -> none  [the longest x1 5.2 us: body(): lax.all_to_all(to_owner(grad_mixed), 'seq', split_axis=2, concat_axis=0,...]
    pallas_call x0 -> x1, Pallas kernels: none -> 23 us  [direct_body(): pl.pallas_call(functools.partial(kernel, (shards, replicas, tokens, own,...]
    all_to_all x6 -> x0, waiting for transfers between devices: 18.4 us -> none  [the longest x1 4.97 us: body(): lax.all_to_all(spread, 'seq', split_axis=1, concat_axis=0, tiled=True)]
    add x3 -> x0, local copies, waits for them, and re-layouts: 8.84 us -> none  [inner_inverse(): out_im = by_outer(cos_outer, turned_im) + by_outer(sin_outer, turned_re)]
    reduce_scatter x1 -> x0, waiting for transfers between devices: 8.45 us -> none  [body(): lax.psum_scatter(per_filter.astype(jnp.bfloat16), 'batch', scatter_dimens...]
    sub x3 -> x0, local copies, waits for them, and re-layouts: 8 us -> none  [inner_inverse(): out_re = by_outer(cos_outer, turned_re) - by_outer(sin_outer, turned_im)]
  transfers between devices with their start and end apart: 7 -> 0, of which waited for: 6 -> 0; matrix products, arithmetic and copies ran while one was open for 11% -> 0% of each run, Pallas kernels for 0% -> 0%
where the time goes in v1:
time: 27.6 us; the launch traced here: 27.3 us
  Pallas kernels  23 us (83%)
  local copies, waits for them, and re-layouts  3.69 us (13%)
  between operations  0.65 us (2%)
    pallas_call x1, Pallas kernels, direct_body(): pl.pallas_call(functools.partial(kernel, (shards, replicas, tokens, own,...  23 us
    unnamed x10, local copies, waits for them, and re-layouts  3.69 us

profile of v1, /device:TPU:0, one launch (start us, length us, event | category | flops | bytes accessed | tf_op | source)
XLA Modules:
  0.0 27.3 jit_solution(16260445717570516024)
XLA Ops:
  0.6 23.0 %shard_map.84 = (bf16[1,256,128]{2,1,0:T(8,128)(2,1)}, bf16[1,256,128]{2,1,0:T(8,128)(2,1)}, bf16[1,256,128]{2,1,0:T(8,128)(2,1)}, f32[16,256]{1,0:T(8,128)}) custom-call(bf16[1,256,128]{2,1,0:T(8,128)(2,1)} %values_ref.1, bf16[1,256,128]{2,1,0:T(8,128)(2,1)} %gate_in_ref.1, bf16[1,256,128]{2,1,0:T(8,128)(2,1)} %gate_out_ref.1, ...), custom_call_target="tpu_custom_call" | custom-call | tf_op jit(solution)/shard_map/pallas_call | solution.py:515
  23.6 0.0 copy-start.1
  23.6 1.5 %copy.13 = bf16[1,256,128]{2,1,0:T(8,128)(2,1)} copy(bf16[1,256,128]{2,1,0:T(8,128)(2,1)} %get-tuple-element.8) | data formatting | bytes 131072
  25.1 0.0 copy-done.1
  25.1 0.0 copy-start
  25.1 0.6 %copy.14 = bf16[1,256,128]{2,1,0:T(8,128)(2,1)} copy(bf16[1,256,128]{2,1,0:T(8,128)(2,1)S(1)} %copy-done.1) | data formatting | bytes 131072
  25.8 0.2 copy-done
  26.0 0.0 copy-start.2
  26.0 0.6 %copy.15 = bf16[1,256,128]{2,1,0:T(8,128)(2,1)} copy(bf16[1,256,128]{2,1,0:T(8,128)(2,1)S(1)} %copy-done) | data formatting | bytes 131072
  26.6 0.1 copy-done.2
  26.7 0.6 %copy.16 = f32[16,256]{1,0:T(8,128)} copy(f32[16,256]{1,0:T(8,128)S(1)} %copy-done.2) | data formatting | bytes 32768
Async XLA Ops:
  23.6 1.5 %copy-start.1 = (bf16[1,256,128]{2,1,0:T(8,128)(2,1)S(1)}, bf16[1,256,128]{2,1,0:T(8,128)(2,1)}, u32[]{:S(2)}) copy-start(bf16[1,256,128]{2,1,0:T(8,128)(2,1)} %get-tuple-element.9) | copy-start | bytes 196612
  25.1 0.9 %copy-start = (bf16[1,256,128]{2,1,0:T(8,128)(2,1)S(1)}, bf16[1,256,128]{2,1,0:T(8,128)(2,1)}, u32[]{:S(2)}) copy-start(bf16[1,256,128]{2,1,0:T(8,128)(2,1)} %get-tuple-element.10) | copy-start | bytes 196612
  26.0 0.7 %copy-start.2 = (f32[16,256]{1,0:T(8,128)S(1)}, f32[16,256]{1,0:T(8,128)}, u32[]{:S(2)}) copy-start(f32[16,256]{1,0:T(8,128)} %get-tuple-element.11) | copy-start | bytes 49156

commit v2 on v1

--- a/solution.py
+++ b/solution.py
@@ -225,10 +225,12 @@
     gate_out_ref,
     cotangent_ref,
     filters_ref,
-    grad_values_ref,
-    grad_gate_in_ref,
-    grad_gate_out_ref,
-    grad_filters_ref,
+    result_held,
+    tap_held,
+    values_here,
+    gate_in_here,
+    gate_out_here,
+    cotangent_here,
     sent,
     held,
     held_taps,
@@ -237,10 +239,8 @@
     padded,
     result,
     result_sent,
-    result_held,
     tap_rows,
     tap_sent,
-    tap_held,
     own_sem,
     in_send,
     in_recv,
@@ -250,6 +250,8 @@
     out_recv,
     term_send,
     term_recv,
+    load_sem,
+    near,
 ):
     shards, replicas, tokens, own, reps, factor = dims
     halves = tokens // LANES
@@ -258,18 +260,39 @@
     group = own * shards
     me = lax.axis_index("seq")
     row = lax.axis_index("batch")
-    flat = me * replicas + row
     f32, bf16 = jnp.float32, jnp.bfloat16
 
     barrier = pltpu.get_barrier_semaphore()
-    for step in range(1, shards * replicas):
-        other = lax.rem(flat + step, shards * replicas)
-        pl.semaphore_signal(
-            barrier,
-            inc=1,
-            device_id={"seq": other // replicas, "batch": lax.rem(other, replicas)},
-            device_id_type=MESH,
-        )
+    peers = [lax.rem(me + step, shards) for step in range(1, shards)]
+    for peer in peers:
+        pl.semaphore_signal(barrier, inc=1, device_id={"seq": peer}, device_id_type=MESH)
+    has_below = row > 0
+    has_above = row < replicas - 1
+    neighbours = has_below.astype(jnp.int32) + has_above.astype(jnp.int32)
+
+    def greet(semaphore):
+        @pl.when(has_below)
+        def _():
+            pl.semaphore_signal(semaphore, inc=1, device_id={"batch": row - 1}, device_id_type=MESH)
+
+        @pl.when(has_above)
+        def _():
+            pl.semaphore_signal(semaphore, inc=1, device_id={"batch": row + 1}, device_id_type=MESH)
+
+    greet(barrier)
+    loads = [
+        pltpu.make_async_copy(source, here, load_sem.at[at])
+        for at, (source, here) in enumerate(
+            (
+                (values_ref, values_here),
+                (gate_in_ref, gate_in_here),
+                (cotangent_ref, cotangent_here),
+                (gate_out_ref, gate_out_here),
+            )
+        )
+    ]
+    for load in loads:
+        load.start()
 
     down = lax.broadcasted_iota(jnp.int32, (LANES, LANES), 0)
     across = lax.broadcasted_iota(jnp.int32, (LANES, LANES), 1)
@@ -279,10 +302,12 @@
     def product(left, right):
         return (left.astype(f32) * right.astype(f32)).astype(bf16)
 
+    for load in loads:
+        load.wait()
     for half in range(halves):
         rows = pl.ds(half * LANES, LANES)
-        mixed = product(values_ref[0, rows, :], gate_in_ref[0, rows, :])
-        grad = product(cotangent_ref[0, rows, :], gate_out_ref[0, rows, :])
+        mixed = product(values_here[0, rows, :], gate_in_here[0, rows, :])
+        grad = product(cotangent_here[0, rows, :], gate_out_here[0, rows, :])
         mixed_t = mixed.astype(f32).T
         grad_t = jnp.dot(mirror, grad, preferred_element_type=f32).T
         for owner in range(shards):
@@ -293,7 +318,9 @@
             ]
             sent[owner, half * lines : (half + 1) * lines, :] = jnp.concatenate(parts, 0).astype(bf16)
 
-    pl.semaphore_wait(barrier, shards * replicas - 1)
+    pl.semaphore_wait(barrier, shards - 1 + neighbours)
+    if replicas > 1:
+        greet(near.at[0])
 
     def taps_copy(source_owner, slot, peer):
         return pltpu.make_async_remote_copy(
@@ -325,27 +352,105 @@
             device_id_type=MESH,
         )
 
-    peers = [lax.rem(me + step, shards) for step in range(1, shards)]
+    for peer in peers:
+        in_copy(peer, me, peer).start()
+    own_in = pltpu.make_async_copy(sent.at[me], held.at[me], own_sem.at[0])
+    own_in.start()
     for peer in peers:
         taps_copy(peer, me, peer).start()
-        in_copy(peer, me, peer).start()
     own_taps = pltpu.make_async_copy(
-        filters_ref.at[pl.ds(pl.multiple_of(me * own, own), own), :], held_taps.at[me], own_sem.at[0]
-    )
-    own_in = pltpu.make_async_copy(sent.at[me], held.at[me], own_sem.at[1])
+        filters_ref.at[pl.ds(pl.multiple_of(me * own, own), own), :], held_taps.at[me], own_sem.at[1]
+    )
     own_taps.start()
-    own_in.start()
     zero_rows = jnp.zeros((blocks, LANES), f32)
     for rep in range(reps):
         padded[rep, 0:blocks, :] = zero_rows
         padded[reps + rep, blocks : 2 * blocks, :] = zero_rows
-    own_taps.wait()
+    for hop in range(1, replicas - 1):
+        pl.semaphore_wait(near.at[hop - 1], neighbours)
+        greet(near.at[hop])
     own_in.wait()
     for peer in peers:
-        taps_copy(peer, peer, peer).wait_recv()
         in_copy(peer, peer, peer).wait_recv()
     for source in range(shards):
         series[source * halves * lines : (source + 1) * halves * lines, :] = held[source].astype(f32)
+
+    def place(f):
+        for line in range(2 * reps):
+            at = 0 if line >= reps else blocks
+            padded[line, at : at + blocks, :] = series[pl.ds(line * own + f, blocks, stride=lines), :]
+
+    def one_gram(f, carry):
+        place(f)
+        grad_cols = jnp.concatenate(
+            [padded[reps + rep, 0:blocks, :] for rep in range(reps)], 0
+        ).T.astype(bf16)
+        gram_before = None
+        for pair in range(blocks // 2):
+            left = jnp.concatenate(
+                [
+                    jnp.concatenate(
+                        [padded[rep, blocks - k : 2 * blocks - k, :] for rep in range(reps)], 0
+                    ).astype(bf16)
+                    for k in (2 * pair, 2 * pair + 1)
+                ],
+                1,
+            )
+            gram = jnp.dot(grad_cols, left, preferred_element_type=f32)
+            for at in range(2):
+                k = 2 * pair + at
+                gram_now = pltpu.roll(
+                    gram[:, at * LANES : (at + 1) * LANES], 0, 1, stride=1, stride_axis=0
+                )
+                if k > 0:
+                    tap_rows[pl.ds((k - 1) * own + f, 1), :] = jnp.sum(
+                        jnp.where(later, gram_before, gram_now), axis=0, keepdims=True
+                    )
+                gram_before = gram_now
+        tap_rows[pl.ds((blocks - 1) * own + f, 1), :] = jnp.sum(
+            jnp.where(later, gram_before, 0.0), axis=0, keepdims=True
+        )
+        return carry
+
+    lax.fori_loop(0, own, one_gram, 0)
+
+    terms = jnp.dot(tap_rows[...].astype(bf16), mirror, preferred_element_type=f32).astype(bf16)
+    for peer in range(shards):
+        tap_sent[peer] = terms[peer * halves * own : (peer + 1) * halves * own]
+
+    per_row = shards // replicas
+    goal = me // per_row
+    slot_here = lax.rem(me, per_row) * replicas + row
+
+    def term_copy(peer, to_row, slot):
+        return pltpu.make_async_remote_copy(
+            src_ref=tap_sent.at[peer],
+            dst_ref=tap_held.at[slot],
+            send_sem=term_send.at[peer],
+            recv_sem=term_recv.at[slot],
+            device_id={"seq": peer, "batch": to_row},
+            device_id_type=MESH,
+        )
+
+    own_term = pltpu.make_async_copy(tap_sent.at[me], tap_held.at[slot_here], own_sem.at[2])
+    stays = goal == row
+    if replicas > 1:
+        pl.semaphore_wait(near.at[replicas - 2], neighbours)
+    for peer in peers:
+        term_copy(peer, goal, slot_here).start()
+
+    @pl.when(stays)
+    def _():
+        own_term.start()
+
+    @pl.when(jnp.logical_not(stays))
+    def _():
+        term_copy(me, goal, slot_here).start()
+
+    own_taps.wait()
+    for peer in peers:
+        taps_copy(peer, peer, peer).wait_recv()
+    for source in range(shards):
         for half in range(halves):
             k = source * halves + half
             taps_rows[k * own : (k + 1) * own, :] = held_taps[
@@ -353,15 +458,9 @@
             ]
 
     def one_filter(f, carry):
-        for line in range(2 * reps):
-            at = 0 if line >= reps else blocks
-            padded[line, at : at + blocks, :] = series[pl.ds(line * own + f, blocks, stride=lines), :]
-        grad_cols = jnp.concatenate(
-            [padded[reps + rep, 0:blocks, :] for rep in range(reps)], 0
-        ).T.astype(bf16)
+        place(f)
         total = jnp.zeros((2 * reps * blocks, LANES), f32)
         turned_before = jnp.zeros((LANES, LANES), f32)
-        gram_before = None
         for pair in range(blocks // 2):
             lefts, rights = [], []
             for k in (2 * pair, 2 * pair + 1):
@@ -376,22 +475,11 @@
                         0,
                     ).astype(bf16)
                 )
-            left = jnp.concatenate(lefts, 1)
-            total = total + jnp.dot(left, jnp.concatenate(rights, 0), preferred_element_type=f32)
-            gram = jnp.dot(grad_cols, left[: reps * blocks], preferred_element_type=f32)
-            for at in range(2):
-                k = 2 * pair + at
-                gram_now = pltpu.roll(
-                    gram[:, at * LANES : (at + 1) * LANES], 0, 1, stride=1, stride_axis=0
-                )
-                if k > 0:
-                    tap_rows[pl.ds((k - 1) * own + f, 1), :] = jnp.sum(
-                        jnp.where(later, gram_before, gram_now), axis=0, keepdims=True
-                    )
-                gram_before = gram_now
-        tap_rows[pl.ds((blocks - 1) * own + f, 1), :] = jnp.sum(
-            jnp.where(later, gram_before, 0.0), axis=0, keepdims=True
-        )
+            total = total + jnp.dot(
+                jnp.concatenate(lefts, 1),
+                jnp.concatenate(rights, 0),
+                preferred_element_type=f32,
+            )
         for line in range(2 * reps):
             result[pl.ds(line * own + f, blocks, stride=lines), :] = total[
                 line * blocks : (line + 1) * blocks
@@ -404,46 +492,57 @@
         result_sent[peer] = result[
             peer * halves * lines : (peer + 1) * halves * lines, :
         ].astype(bf16)
-    terms = jnp.dot(tap_rows[...].astype(bf16), mirror, preferred_element_type=f32).astype(bf16)
-    for peer in range(shards):
-        tap_sent[peer] = terms[peer * halves * own : (peer + 1) * halves * own]
-
     for peer in peers:
         out_copy(me, peer).start()
     own_out = pltpu.make_async_copy(result_sent.at[me], result_held.at[me], own_sem.at[0])
     own_out.start()
-
-    per_row = shards // replicas
-    goal = me // per_row
-    slot_here = lax.rem(me, per_row) * replicas + row
-
-    def term_copy(peer, to_row, slot):
-        return pltpu.make_async_remote_copy(
-            src_ref=tap_sent.at[peer],
-            dst_ref=tap_held.at[slot],
-            send_sem=term_send.at[peer],
-            recv_sem=term_recv.at[slot],
-            device_id={"seq": peer, "batch": to_row},
-            device_id_type=MESH,
-        )
-
-    own_term = pltpu.make_async_copy(tap_sent.at[me], tap_held.at[slot_here], own_sem.at[1])
-    stays = goal == row
-    for peer in peers:
-        term_copy(peer, goal, slot_here).start()
-
-    @pl.when(stays)
-    def _():
-        own_term.start()
+    own_out.wait()
+    for peer in peers:
+        out_copy(peer, peer).wait_recv()
+
+    for at in range(per_row):
+        for source_row in range(replicas):
+            slot = at * replicas + source_row
+            local = jnp.logical_and(me == row * per_row + at, row == source_row)
+
+            @pl.when(local)
+            def _():
+                own_term.wait()
+
+            @pl.when(jnp.logical_not(local))
+            def _(slot=slot):
+                term_copy(me, row, slot).wait_recv()
+
+    for peer in peers:
+        taps_copy(peer, me, peer).wait_send()
+        in_copy(peer, me, peer).wait_send()
+        out_copy(me, peer).wait_send()
+        term_copy(peer, goal, slot_here).wait_send()
 
     @pl.when(jnp.logical_not(stays))
     def _():
-        term_copy(me, goal, slot_here).start()
-
-    own_out.wait()
-    for peer in peers:
-        out_copy(peer, peer).wait_recv()
-
+        term_copy(me, goal, slot_here).wait_send()
+
+
+def finish(
+    dims,
+    values_ref,
+    gate_in_ref,
+    cotangent_ref,
+    result_held,
+    tap_held,
+    grad_values_ref,
+    grad_gate_in_ref,
+    grad_gate_out_ref,
+    grad_filters_ref,
+):
+    shards, replicas, tokens, own, reps, factor = dims
+    halves = tokens // LANES
+    lines = 2 * reps * own
+    f32, bf16 = jnp.float32, jnp.bfloat16
+    down = lax.broadcasted_iota(jnp.int32, (LANES, LANES), 0)
+    across = lax.broadcasted_iota(jnp.int32, (LANES, LANES), 1)
+    mirror = jnp.where(down + across == LANES - 1, 1.0, 0.0).astype(bf16)
     for half in range(halves):
         rows = pl.ds(half * LANES, LANES)
         moved = []
@@ -463,21 +562,7 @@
         grad_values_ref[0, rows, :] = (gate_in_ref[0, rows, :].astype(f32) * back).astype(bf16)
         grad_gate_in_ref[0, rows, :] = (values_ref[0, rows, :].astype(f32) * back).astype(bf16)
         grad_gate_out_ref[0, rows, :] = (cotangent_ref[0, rows, :].astype(f32) * conv).astype(bf16)
-
-    for at in range(per_row):
-        for source_row in range(replicas):
-            slot = at * replicas + source_row
-            local = jnp.logical_and(me == row * per_row + at, row == source_row)
-
-            @pl.when(local)
-            def _():
-                own_term.wait()
-
-            @pl.when(jnp.logical_not(local))
-            def _(slot=slot):
-                term_copy(me, row, slot).wait_recv()
-
-    for at in range(per_row):
+    for at in range(shards // replicas):
         summed = sum(
             tap_held[at * replicas + source_row].astype(f32) for source_row in range(replicas)
         )
@@ -485,16 +570,6 @@
             grad_filters_ref[at * own : (at + 1) * own, half * LANES : (half + 1) * LANES] = (
                 summed[half * own : (half + 1) * own] * factor
             )
-
-    for peer in peers:
-        taps_copy(peer, me, peer).wait_send()
-        in_copy(peer, me, peer).wait_send()
-        out_copy(me, peer).wait_send()
-        term_copy(peer, goal, slot_here).wait_send()
-
-    @pl.when(jnp.logical_not(stays))
-    def _():
-        term_copy(me, goal, slot_here).wait_send()
 
 
 def direct_body(values, gate_in, gate_out, cotangent, filters):
@@ -509,11 +584,40 @@
     lines = 2 * reps * own
     factor = 1.0 / math.sqrt(reps * replicas * shards * tokens)
     vmem = pl.BlockSpec(memory_space=pltpu.VMEM)
+    anywhere = pl.BlockSpec(memory_space=pl.ANY)
     f32, bf16 = jnp.float32, jnp.bfloat16
     slab = jax.ShapeDtypeStruct(values.shape, bf16)
     sems = pltpu.SemaphoreType.DMA((shards,))
+    dims = (shards, replicas, tokens, own, reps, factor)
+    message = (shards, halves * lines, LANES)
+    results, terms = pl.pallas_call(
+        functools.partial(kernel, dims),
+        out_shape=(
+            jax.ShapeDtypeStruct(message, bf16),
+            jax.ShapeDtypeStruct((shards, halves * own, LANES), bf16),
+        ),
+        in_specs=[anywhere] * 5,
+        out_specs=(anywhere,) * 2,
+        scratch_shapes=[pltpu.VMEM(values.shape, bf16)] * 4
+        + [
+            pltpu.VMEM(message, bf16),
+            pltpu.VMEM(message, bf16),
+            pltpu.VMEM((shards, own, tokens), f32),
+            pltpu.VMEM((blocks * own + 8, LANES), f32),
+            pltpu.VMEM((blocks * lines, LANES), f32),
+            pltpu.VMEM((2 * reps, 2 * blocks, LANES), f32),
+            pltpu.VMEM((blocks * lines, LANES), f32),
+            pltpu.VMEM(message, bf16),
+            pltpu.VMEM((blocks * own, LANES), f32),
+            pltpu.VMEM((shards, halves * own, LANES), bf16),
+            pltpu.SemaphoreType.DMA((3,)),
+        ]
+        + [sems] * 8
+        + [pltpu.SemaphoreType.DMA((4,)), pltpu.SemaphoreType.REGULAR((max(replicas - 1, 1),))],
+        compiler_params=pltpu.CompilerParams(collective_id=0, has_side_effects=True),
+    )(values, gate_in, gate_out, cotangent, filters)
     return pl.pallas_call(
-        functools.partial(kernel, (shards, replicas, tokens, own, reps, factor)),
+        functools.partial(finish, dims),
         out_shape=(
             slab,
             slab,
@@ -522,24 +626,7 @@
         ),
         in_specs=[vmem] * 5,
         out_specs=(vmem,) * 4,
-        scratch_shapes=[
-            pltpu.VMEM((shards, halves * lines, LANES), bf16),
-            pltpu.VMEM((shards, halves * lines, LANES), bf16),
-            pltpu.VMEM((shards, own, tokens), f32),
-            pltpu.VMEM((blocks * own + 8, LANES), f32),
-            pltpu.VMEM((blocks * lines, LANES), f32),
-            pltpu.VMEM((2 * reps, 2 * blocks, LANES), f32),
-            pltpu.VMEM((blocks * lines, LANES), f32),
-            pltpu.VMEM((shards, halves * lines, LANES), bf16),
-            pltpu.VMEM((shards, halves * lines, LANES), bf16),
-            pltpu.VMEM((blocks * own, LANES), f32),
-            pltpu.VMEM((shards, halves * own, LANES), bf16),
-            pltpu.VMEM((shards, halves * own, LANES), bf16),
-            pltpu.SemaphoreType.DMA((2,)),
-        ]
-        + [sems] * 8,
-        compiler_params=pltpu.CompilerParams(collective_id=0, has_side_effects=True),
-    )(values, gate_in, gate_out, cotangent, filters)
+    )(values, gate_in, cotangent, results, terms)
 
 
 def body(values, gate_in, gate_out, cotangent, filters):

time: 27.6 us -> 22.8 us (0.83)
  local copies, waits for them, and re-layouts: 3.69 us -> 0 us
  Pallas kernels: 23 us -> 22 us
    unnamed x10 -> x0, local copies, waits for them, and re-layouts: 3.69 us -> none
    pallas_call x1 -> x2, Pallas kernels: 23 us -> 22 us  [the longest x1 20.1 us: direct_body(): pl.pallas_call(functools.partial(kernel, dims), out_shape=(jax.ShapeDtype...]
where the time goes in v2:
time: 22.8 us; the launch traced here: 22.6 us
  Pallas kernels  22 us (96%)
  between operations  0.64 us (3%)
    pallas_call x1, Pallas kernels, direct_body(): pl.pallas_call(functools.partial(kernel, dims), out_shape=(jax.ShapeDtype...  20.1 us
    pallas_call x1, Pallas kernels, direct_body(): pl.pallas_call(functools.partial(finish, dims), out_shape=(slab, slab, sl...  1.89 us

profile of v2, /device:TPU:0, one launch (start us, length us, event | category | flops | bytes accessed | tf_op | source)
XLA Modules:
  0.0 22.6 jit_solution(5874133504464313245)
XLA Ops:
  0.6 20.1 %shard_map.84 = (bf16[8,64,128]{2,1,0:T(8,128)(2,1)}, bf16[8,16,128]{2,1,0:T(8,128)(2,1)}) custom-call(bf16[1,256,128]{2,1,0:T(8,128)(2,1)} %values_ref.3, bf16[1,256,128]{2,1,0:T(8,128)(2,1)} %gate_in_ref.3, bf16[1,256,128]{2,1,0:T(8,128)(2,1)} %gate_out_ref.1, bf16[1,256,128]{2,1,0:T(8,128)(2,1)} %cotangent_ref.3, f32[64,256]{1,0:T(8,128)} %filters_ref.1), custom_call_target="tpu_custom_call" | custom-call | tf_op jit(solution)/shard_map/pallas_call | solution.py:593
  20.7 1.9 %shard_map.85 = (bf16[1,256,128]{2,1,0:T(8,128)(2,1)}, bf16[1,256,128]{2,1,0:T(8,128)(2,1)}, bf16[1,256,128]{2,1,0:T(8,128)(2,1)}, f32[16,256]{1,0:T(8,128)}) custom-call(bf16[1,256,128]{2,1,0:T(8,128)(2,1)} %values_ref.3, bf16[1,256,128]{2,1,0:T(8,128)(2,1)} %gate_in_ref.3, bf16[1,256,128]{2,1,0:T(8,128)(2,1)} %cotangent_ref.3, ...), custom_call_target="tpu_custom_call" | custom-call | tf_op jit(solution)/shard_map/pallas_call | solution.py:619

commit v3 on v2

--- a/solution.py
+++ b/solution.py
@@ -215,6 +215,8 @@
 
 
 LANES = 128
+SHIFTS = 4
+BANKS = 4
 MESH = pl.DeviceIdType.MESH
 
 
@@ -237,6 +239,8 @@
     taps_rows,
     series,
     padded,
+    shifted,
+    carried,
     result,
     result_sent,
     tap_rows,
@@ -263,7 +267,15 @@
     f32, bf16 = jnp.float32, jnp.bfloat16
 
     barrier = pltpu.get_barrier_semaphore()
-    peers = [lax.rem(me + step, shards) for step in range(1, shards)]
+    if shards & (shards - 1) == 0:
+        digits = [1 << at for at in range(shards.bit_length() - 1)]
+        flips = {digit: digit - 2 * digit * lax.rem(me // digit, 2) for digit in digits}
+        peers = [
+            me + sum(flips[digit] for digit in digits if mask & digit)
+            for mask in range(shards - 1, 0, -1)
+        ]
+    else:
+        peers = [lax.rem(me + step, shards) for step in range(1, shards)]
     for peer in peers:
         pl.semaphore_signal(barrier, inc=1, device_id={"seq": peer}, device_id_type=MESH)
     has_below = row > 0
@@ -363,34 +375,59 @@
     )
     own_taps.start()
     zero_rows = jnp.zeros((blocks, LANES), f32)
-    for rep in range(reps):
-        padded[rep, 0:blocks, :] = zero_rows
-        padded[reps + rep, blocks : 2 * blocks, :] = zero_rows
-    for hop in range(1, replicas - 1):
+    for bank in range(BANKS):
+        for rep in range(reps):
+            padded[bank, rep, 0:blocks, :] = zero_rows
+            padded[bank, reps + rep, blocks : 2 * blocks, :] = zero_rows
+    for hop in range(1, min(2, replicas - 1)):
         pl.semaphore_wait(near.at[hop - 1], neighbours)
         greet(near.at[hop])
     own_in.wait()
     for peer in peers:
         in_copy(peer, peer, peer).wait_recv()
+    for hop in range(2, replicas - 1):
+        pl.semaphore_wait(near.at[hop - 1], neighbours)
+        greet(near.at[hop])
     for source in range(shards):
         series[source * halves * lines : (source + 1) * halves * lines, :] = held[source].astype(f32)
 
-    def place(f):
+    def place(f, padded):
         for line in range(2 * reps):
             at = 0 if line >= reps else blocks
             padded[line, at : at + blocks, :] = series[pl.ds(line * own + f, blocks, stride=lines), :]
 
-    def one_gram(f, carry):
-        place(f)
+    fine = LANES // SHIFTS
+    later_fine = later[:fine]
+    for bank in range(BANKS):
+        carried[bank, 0:8, :] = jnp.zeros((8, LANES), f32)
+
+    def one_gram(f, padded, shifted, carried):
+        place(f, padded)
         grad_cols = jnp.concatenate(
             [padded[reps + rep, 0:blocks, :] for rep in range(reps)], 0
-        ).T.astype(bf16)
+        ).T
+        grad_cols = jnp.concatenate(
+            [grad_cols[shift * fine : (shift + 1) * fine] for shift in range(SHIFTS)], 1
+        ).astype(bf16)
+        for shift in range(1, SHIFTS):
+            for rep in range(reps):
+                turned = pltpu.roll(padded[rep], shift * fine, 1)
+                carried[8 : 8 + 2 * blocks, :] = turned
+                wide = lax.broadcasted_iota(jnp.int32, turned.shape, 1) >= shift * fine
+                shifted[(shift - 1) * reps + rep] = jnp.where(
+                    wide, turned, carried[7 : 7 + 2 * blocks, :]
+                )
         gram_before = None
         for pair in range(blocks // 2):
             left = jnp.concatenate(
                 [
                     jnp.concatenate(
-                        [padded[rep, blocks - k : 2 * blocks - k, :] for rep in range(reps)], 0
+                        [padded[rep, blocks - k : 2 * blocks - k, :] for rep in range(reps)]
+                        + [
+                            shifted[at, blocks - k : 2 * blocks - k, :]
+                            for at in range((SHIFTS - 1) * reps)
+                        ],
+                        0,
                     ).astype(bf16)
                     for k in (2 * pair, 2 * pair + 1)
                 ],
@@ -404,15 +441,18 @@
                 )
                 if k > 0:
                     tap_rows[pl.ds((k - 1) * own + f, 1), :] = jnp.sum(
-                        jnp.where(later, gram_before, gram_now), axis=0, keepdims=True
+                        jnp.where(later_fine, gram_before, gram_now), axis=0, keepdims=True
                     )
                 gram_before = gram_now
         tap_rows[pl.ds((blocks - 1) * own + f, 1), :] = jnp.sum(
-            jnp.where(later, gram_before, 0.0), axis=0, keepdims=True
-        )
-        return carry
-
-    lax.fori_loop(0, own, one_gram, 0)
+            jnp.where(later_fine, gram_before, 0.0), axis=0, keepdims=True
+        )
+
+    @pl.loop(0, own // BANKS)
+    def _(at):
+        for bank in range(BANKS):
+            one_gram(at * BANKS + bank, padded.at[bank], shifted.at[bank], carried.at[bank])
+
 
     terms = jnp.dot(tap_rows[...].astype(bf16), mirror, preferred_element_type=f32).astype(bf16)
     for peer in range(shards):
@@ -457,8 +497,8 @@
                 source, :, half * LANES : (half + 1) * LANES
             ]
 
-    def one_filter(f, carry):
-        place(f)
+    def one_filter(f, padded):
+        place(f, padded)
         total = jnp.zeros((2 * reps * blocks, LANES), f32)
         turned_before = jnp.zeros((LANES, LANES), f32)
         for pair in range(blocks // 2):
@@ -484,9 +524,12 @@
             result[pl.ds(line * own + f, blocks, stride=lines), :] = total[
                 line * blocks : (line + 1) * blocks
             ]
-        return carry
-
-    lax.fori_loop(0, own, one_filter, 0)
+
+    @pl.loop(0, own // BANKS)
+    def _(at):
+        for bank in range(BANKS):
+            one_filter(at * BANKS + bank, padded.at[bank])
+
 
     for peer in range(shards):
         result_sent[peer] = result[
@@ -605,7 +648,9 @@
             pltpu.VMEM((shards, own, tokens), f32),
             pltpu.VMEM((blocks * own + 8, LANES), f32),
             pltpu.VMEM((blocks * lines, LANES), f32),
-            pltpu.VMEM((2 * reps, 2 * blocks, LANES), f32),
+            pltpu.VMEM((BANKS, 2 * reps, 2 * blocks, LANES), f32),
+            pltpu.VMEM((BANKS, (SHIFTS - 1) * reps, 2 * blocks, LANES), f32),
+            pltpu.VMEM((BANKS, 8 + 2 * blocks, LANES), f32),
             pltpu.VMEM((blocks * lines, LANES), f32),
             pltpu.VMEM(message, bf16),
             pltpu.VMEM((blocks * own, LANES), f32),

time: 22.8 us -> 18.3 us (0.80)
  Pallas kernels: 22 us -> 17.5 us
    pallas_call x1, Pallas kernels: 20.1 us -> 15.6 us  [direct_body(): pl.pallas_call(functools.partial(kernel, dims), out_shape=(jax.ShapeDtype...]
where the time goes in v3:
time: 18.3 us; the launch traced here: 18.1 us
  Pallas kernels  17.5 us (96%)
  between operations  0.64 us (3%)
    pallas_call x1, Pallas kernels, direct_body(): pl.pallas_call(functools.partial(kernel, dims), out_shape=(jax.ShapeDtype...  15.6 us
    pallas_call x1, Pallas kernels, direct_body(): pl.pallas_call(functools.partial(finish, dims), out_shape=(slab, slab, sl...  1.89 us

profile of v3, /device:TPU:0, one launch (start us, length us, event | category | flops | bytes accessed | tf_op | source)
XLA Modules:
  0.0 18.1 jit_solution(17351618827604211174)
XLA Ops:
  0.6 15.6 %shard_map.84 = (bf16[8,64,128]{2,1,0:T(8,128)(2,1)}, bf16[8,16,128]{2,1,0:T(8,128)(2,1)}) custom-call(bf16[1,256,128]{2,1,0:T(8,128)(2,1)} %values_ref.3, bf16[1,256,128]{2,1,0:T(8,128)(2,1)} %gate_in_ref.3, bf16[1,256,128]{2,1,0:T(8,128)(2,1)} %gate_out_ref.1, bf16[1,256,128]{2,1,0:T(8,128)(2,1)} %cotangent_ref.3, f32[64,256]{1,0:T(8,128)} %filters_ref.1), custom_call_target="tpu_custom_call" | custom-call | tf_op jit(solution)/shard_map/pallas_call | solution.py:636
  16.2 1.9 %shard_map.85 = (bf16[1,256,128]{2,1,0:T(8,128)(2,1)}, bf16[1,256,128]{2,1,0:T(8,128)(2,1)}, bf16[1,256,128]{2,1,0:T(8,128)(2,1)}, f32[16,256]{1,0:T(8,128)}) custom-call(bf16[1,256,128]{2,1,0:T(8,128)(2,1)} %values_ref.3, bf16[1,256,128]{2,1,0:T(8,128)(2,1)} %gate_in_ref.3, bf16[1,256,128]{2,1,0:T(8,128)(2,1)} %cotangent_ref.3, ...), custom_call_target="tpu_custom_call" | custom-call | tf_op jit(solution)/shard_map/pallas_call | solution.py:664

commit v4 on v3

--- a/solution.py
+++ b/solution.py
@@ -216,7 +216,7 @@
 
 LANES = 128
 SHIFTS = 4
-BANKS = 4
+BANKS = 8
 MESH = pl.DeviceIdType.MESH
 
 

time: 18.3 us -> 18.1 us (0.989)
  Pallas kernels: 17.5 us -> 17.3 us
    pallas_call x1, Pallas kernels: 15.6 us -> 15.4 us  [direct_body(): pl.pallas_call(functools.partial(kernel, dims), out_shape=(jax.ShapeDtype...]
where the time goes in v4:
time: 18.1 us; the launch traced here: 17.9 us
  Pallas kernels  17.3 us (96%)
  between operations  0.64 us (4%)
    pallas_call x1, Pallas kernels, direct_body(): pl.pallas_call(functools.partial(kernel, dims), out_shape=(jax.ShapeDtype...  15.4 us
    pallas_call x1, Pallas kernels, direct_body(): pl.pallas_call(functools.partial(finish, dims), out_shape=(slab, slab, sl...  1.89 us

profile of v4, /device:TPU:0, one launch (start us, length us, event | category | flops | bytes accessed | tf_op | source)
XLA Modules:
  0.0 17.9 jit_solution(9408581008250400832)
XLA Ops:
  0.6 15.4 %shard_map.84 = (bf16[8,64,128]{2,1,0:T(8,128)(2,1)}, bf16[8,16,128]{2,1,0:T(8,128)(2,1)}) custom-call(bf16[1,256,128]{2,1,0:T(8,128)(2,1)} %values_ref.3, bf16[1,256,128]{2,1,0:T(8,128)(2,1)} %gate_in_ref.3, bf16[1,256,128]{2,1,0:T(8,128)(2,1)} %gate_out_ref.1, bf16[1,256,128]{2,1,0:T(8,128)(2,1)} %cotangent_ref.3, f32[64,256]{1,0:T(8,128)} %filters_ref.1), custom_call_target="tpu_custom_call" | custom-call | tf_op jit(solution)/shard_map/pallas_call | solution.py:636
  16.0 1.9 %shard_map.85 = (bf16[1,256,128]{2,1,0:T(8,128)(2,1)}, bf16[1,256,128]{2,1,0:T(8,128)(2,1)}, bf16[1,256,128]{2,1,0:T(8,128)(2,1)}, f32[16,256]{1,0:T(8,128)}) custom-call(bf16[1,256,128]{2,1,0:T(8,128)(2,1)} %values_ref.3, bf16[1,256,128]{2,1,0:T(8,128)(2,1)} %gate_in_ref.3, bf16[1,256,128]{2,1,0:T(8,128)(2,1)} %cotangent_ref.3, ...), custom_call_target="tpu_custom_call" | custom-call | tf_op jit(solution)/shard_map/pallas_call | solution.py:664
